TPU v7x, 32 devices: a whole 2x2x4 slice. The times are simulated.
32 devices in a mesh: grp: 4 (over y, x), lm: 8 (over z, core).
Axes of the slice: x: 2, y: 2, z: 4, core: 2. Of those that a mesh axis runs over, the one named last changes fastest.
Arguments:
- embeddings: bfloat16 [8192, 512], P(('grp', 'lm')), may hold values from -14 to 14
- landmarks: bfloat16 [16384, 512], P('lm'), may hold values from -14 to 14
- start_vectors: float32 [8192, 128], P(('grp', 'lm')), may hold values from -10 to 10
- row_weight: float32 [8192], P(('grp', 'lm')), may hold values from 0.1 to 9
- spread: float32 [1], replicated, may hold values from 11.313708 to 33.941124
Outputs:
- subspace: float32 [8192, 128], P(('grp', 'lm'))
All inputs are finite; a program needn't handle non-finite values.
Results may differ from a plain program's by a relative error of at most 0.019.
Values may be sent and summed in bfloat16 or wider, within the bound.
A program may use at most 128 MiB of HBM per device.

v0:
```python
import jax
import jax.numpy as jnp
from jax import lax
from jax.sharding import PartitionSpec as P

ITERS = 2


def unit_rows(values):
    values = values.astype(jnp.float32)
    scale = lax.rsqrt(jnp.sum(values * values, axis=1, keepdims=True) + 1e-06)
    return (values * scale).astype(jnp.bfloat16)


def kernel_values(rows_unit, marks_unit, gamma):
    cosine = jnp.einsum("rd,ld->rl", rows_unit, marks_unit, preferred_element_type=jnp.float32)
    return jnp.exp(gamma * cosine)


def local(embeddings, landmarks, start_vectors, row_weight, spread):
    own_rows = embeddings.shape[0]
    marks = landmarks.shape[0]
    groups = lax.axis_size("grp")
    members = lax.axis_size("lm")
    total_rows = own_rows * groups * members
    group_rows = own_rows * members
    gamma = spread[0]
    rows_unit = unit_rows(embeddings)
    marks_unit = unit_rows(landmarks)
    sums = jnp.zeros((marks,), jnp.float32)
    weights = jnp.zeros((group_rows,), jnp.float32)
    part_rows = lax.all_gather(rows_unit, "lm", axis=0, tiled=True)
    part_weight = lax.all_gather(row_weight.astype(jnp.bfloat16), "lm", axis=0, tiled=True).astype(
        jnp.float32
    )
    values = kernel_values(part_rows, marks_unit, gamma)
    build_tile = values.astype(jnp.bfloat16)
    weights = lax.dynamic_update_slice_in_dim(weights, part_weight, jnp.int32(0), 0)
    sums = sums + jnp.sum(part_weight[:, None] * values, axis=0)
    mean_sum, weight_sum = lax.psum((sums, jnp.sum(weights)), "grp")
    means = mean_sum / weight_sum
    vectors = start_vectors
    weighted_full = row_weight[:, None] * vectors
    totals = lax.psum(jnp.sum(weighted_full, axis=0), ("grp", "lm"))
    group_weighted = lax.all_gather(weighted_full.astype(jnp.bfloat16), "lm", axis=0, tiled=True)
    for step in range(ITERS):
        side = (
            lax.psum(
                jnp.einsum(
                    "rl,rv->lv", build_tile, group_weighted, preferred_element_type=jnp.float32
                ),
                "grp",
            )
            - means[:, None] * totals[None, :]
        )
        side_b = side.astype(jnp.bfloat16)
        shift = jnp.dot(means, side_b.astype(jnp.float32), precision=lax.Precision.HIGHEST)
        partial_rows = weights[:, None] * (
            jnp.dot(build_tile, side_b, preferred_element_type=jnp.float32) - shift[None, :]
        )
        image = lax.psum(partial_rows, "lm")
        square, column = lax.psum(
            (jnp.sum(image * image, axis=0), jnp.sum(weights[:, None] * image, axis=0)), "grp"
        )
        scale = jnp.sqrt(square / total_rows + 1e-06)
        group_vectors = image / scale[None, :]
        totals = column / scale
        group_weighted = (weights[:, None] * group_vectors).astype(jnp.bfloat16)
        vectors = lax.dynamic_slice_in_dim(
            group_vectors, lax.axis_index("lm") * own_rows, own_rows, 0
        )
    return vectors


def solution(mesh):
    in_specs = (
        P(("grp", "lm"), None),
        P("lm", None),
        P(("grp", "lm"), None),
        P(("grp", "lm")),
        P(),
    )
    out_specs = P(("grp", "lm"), None)
    return jax.shard_map(local, mesh=mesh, in_specs=in_specs, out_specs=out_specs, check_vma=False)
```

profile of v0, /device:TPU:0, one launch (start us, length us, event | category | flops | bytes accessed | tf_op | source)
XLA Modules:
  0.0 337.8 jit_solution(3544346859675565320)
XLA Ops:
  6.5 0.0 all-gather.3.cloned.1.call-start
  6.5 1.1 fusion.8
  7.6 1.8 fusion.9
  9.4 0.0 all-gather.3.cloned.1.call-update
  9.4 0.0 all-reduce.7.cloned.1.call-start
  9.5 0.7 convert_element_type.35
  10.2 13.5 %all-gather = bf16[8,1,256]{2,1,0:T(2,128)(2,1)S(1)} all-gather(bf16[1,1,256]{2,1,0:T(2,128)(2,1)S(1)} %reshape.21), channel_id=1, replica_groups=mesh['grp'=4,'lm'=8] {'lm'}, dimensions={0}, use_global_device_ids=true | all-gather | bytes 4608 | tf_op jit(solution)/shard_map/all_gather | solution.py:33
  24.3 2.1 fusion.1
  26.4 1.0 multiply_reduce_fusion.4
  27.4 17.3 %all_gather.11 = bf16[2048,128]{1,0:T(8,128)(2,1)S(1)} all-gather(bf16[256,128]{1,0:T(8,128)(2,1)S(1)} %get-tuple-element.14), channel_id=1, replica_groups=mesh['grp'=4,'lm'=8] {'lm'}, dimensions={0}, use_global_device_ids=true | all-gather | bytes 589824 | tf_op jit(solution)/shard_map/all_gather | solution.py:45
  44.7 1.0 all-gather.3.cloned.1.call-done
  45.7 7.8 %multiply_reduce_fusion = (f32[2048]{0:T(1024)S(1)}, bf16[2048,2048]{1,0:T(8,128)(2,1)S(1)}) fusion(f32[2048]{0:T(1024)S(1)} %bitcast.19, f32[]{:T(128)} %bitcast.16, bf16[2048,512]{1,0:T(8,128)(2,1)} %all-gather.3.cloned.1.call-done, bf16[2048,512]{1,0:T(8,128)(2,1)} %param.6, f32[2048]{0:T(1024)S(1)} %add_rsqrt_fusion), kind=kOutput, calls=%fused_computation | convolution fusion | flops 4314888192 | bytes 12607492 | tf_op jit(solution)/shard_map/rd,ld->rl/dot_general | solution.py:16
  53.5 0.0 copy-start
  53.5 3.2 copy-done
  56.7 3.4 %fusion.14 = f32[2048,128]{1,0:T(8,128)} fusion(bf16[2048,2048]{1,0:T(8,128)(2,1)S(1)} %get-tuple-element.12, bf16[2048,128]{1,0:T(8,128)(2,1)S(1)} %all_gather.11), kind=kOutput, calls=%fused_computation.38 | convolution fusion | flops 1073741824 | bytes 9961472 | tf_op jit(solution)/shard_map/rl,rv->lv/dot_general | solution.py:49
  60.2 0.0 all-reduce.7.cloned.1.call-update
  60.2 0.0 all-reduce.9.cloned.1.call-start
  60.2 40.3 %psum.73 = f32[128]{0:T(128)S(1)} all-reduce(f32[128]{0:T(128)S(1)} %get-tuple-element.13), channel_id=1, replica_groups=mesh['grp'=4,'lm'=8] {'grp','lm'}, use_global_device_ids=true, to_apply=%region_8.0 | all-reduce | flops 128 | bytes 1024 | tf_op jit(solution)/shard_map/psum | solution.py:44
  100.5 0.6 convert_reduce_fusion
  101.1 11.7 %all-reduce.1 = (f32[2048]{0:T(1024)S(1)}, f32[]{:T(128)}) all-reduce(f32[2048]{0:T(1024)S(1)} %get-tuple-element.11, f32[]{:T(128)} %convert_reduce_fusion), channel_id=1, replica_groups=mesh['grp'=4,'lm'=8] {'grp'}, use_global_device_ids=true, to_apply=%region_4.0 | all-reduce | flops 2049 | bytes 16392 | tf_op jit(solution)/shard_map/psum | solution.py:40
  112.8 0.6 broadcast_divide_fusion
  113.5 0.0 all-reduce.7.cloned.1.call-done
  113.5 1.8 convolution_bitcast_fusion.1
  115.3 7.1 %fusion.4 = f32[2048,128]{1,0:T(8,128)} fusion(bf16[2048,2048]{1,0:T(8,128)(2,1)} %copy-done, f32[128]{0:T(128)S(1)} %convolution_bitcast_fusion.1, f32[2048]{0:T(1024)S(1)} %bitcast.20, f32[2048,128]{1,0:T(8,128)} %all-reduce.7.cloned.1.call-done, f32[128]{0:T(128)S(1)} %psum.73, f32[2048]{0:T(1024)S(1)} %broadcast_divide_fusion), kind=kOutput, calls=%fused_computation.10 | convolution fusion | flops 1075052544 | bytes 10503168 | tf_op jit(solution)/shard_map/dot_general | solution.py:59
  122.4 0.0 all-reduce.9.cloned.1.call-update
  122.4 0.0 all-reduce.11.cloned.1.call-start
  122.5 58.7 %all-reduce.9.cloned.1.call-done = f32[2048,128]{1,0:T(8,128)} async-done(((f32[2048,128]{1,0:T(8,128)}), f32[2048,128]{1,0:T(8,128)}) %all-reduce.9.cloned.1.call-update) | async-done | bytes 1048592 | tf_op jit(solution)/shard_map/psum | solution.py:61
  181.1 1.6 multiply_reduce_fusion.2
  182.7 10.0 %all-reduce = (f32[128]{0:T(128)S(1)}, f32[128]{0:T(128)S(1)}) all-reduce(f32[128]{0:T(128)S(1)} %get-tuple-element.6, f32[128]{0:T(128)S(1)} %get-tuple-element.5), channel_id=1, replica_groups=mesh['grp'=4,'lm'=8] {'grp'}, use_global_device_ids=true, to_apply=%region_11.0 | all-reduce | flops 256 | bytes 2048 | tf_op jit(solution)/shard_map/psum | solution.py:62
  192.7 7.3 %fusion.10 = f32[2048,128]{1,0:T(8,128)} fusion(bf16[2048,2048]{1,0:T(8,128)(2,1)} %copy-done, f32[2048,128]{1,0:T(8,128)} %all-reduce.9.cloned.1.call-done, f32[128]{0:T(128)S(1)} %get-tuple-element.16, f32[2048]{0:T(1024)S(1)} %bitcast.22), kind=kOutput, calls=%fused_computation.25 | convolution fusion | flops 1074528256 | bytes 10494464 | tf_op jit(solution)/shard_map/rl,rv->lv/dot_general | solution.py:49
  200.0 0.0 all-reduce.11.cloned.1.call-update
  200.0 0.0 all-reduce.13.cloned.1.call-start
  200.1 49.9 %all-reduce.11.cloned.1.call-done = f32[2048,128]{1,0:T(8,128)} async-done(((f32[2048,128]{1,0:T(8,128)}), f32[2048,128]{1,0:T(8,128)}) %all-reduce.11.cloned.1.call-update) | async-done | bytes 1048592 | tf_op jit(solution)/shard_map/psum | solution.py:48
  250.0 1.8 convolution_bitcast_fusion
  251.8 7.1 %fusion.3 = f32[2048,128]{1,0:T(8,128)} fusion(bf16[2048,2048]{1,0:T(8,128)(2,1)} %copy-done, f32[128]{0:T(128)S(1)} %convolution_bitcast_fusion, f32[2048]{0:T(1024)S(1)} %bitcast.23, f32[2048,128]{1,0:T(8,128)} %all-reduce.11.cloned.1.call-done, f32[128]{0:T(128)S(1)} %get-tuple-element.15, f32[2048]{0:T(1024)S(1)} %broadcast_divide_fusion), kind=kOutput, calls=%fused_computation.8 | convolution fusion | flops 1075052544 | bytes 10503168 | tf_op jit(solution)/shard_map/dot_general | solution.py:59
  258.9 0.0 all-reduce.13.cloned.1.call-update
  258.9 59.5 %all-reduce.13.cloned.1.call-done = f32[2048,128]{1,0:T(8,128)} async-done(((f32[2048,128]{1,0:T(8,128)}), f32[2048,128]{1,0:T(8,128)}) %all-reduce.13.cloned.1.call-update) | async-done | bytes 1048592 | tf_op jit(solution)/shard_map/psum | solution.py:61
  318.4 1.5 multiply_reduce_fusion.1
  319.9 9.8 %psum.79 = f32[128]{0:T(128)S(1)} all-reduce(f32[128]{0:T(128)S(1)} %multiply_reduce_fusion.1), channel_id=1, replica_groups=mesh['grp'=4,'lm'=8] {'grp'}, use_global_device_ids=true, to_apply=%region_17.0 | all-reduce | flops 128 | bytes 1024 | tf_op jit(solution)/shard_map/psum | solution.py:62
  329.7 1.6 dynamic-slice_divide_fusion
  (6 shorter events, 0.1 us)
Async XLA Ops:
  6.5 39.1 %all-gather.3.cloned.1.call-start = ((), (), s32[]{:S(2)}) async-start(), calls=%async_computation | async-start | bytes 2359296 | tf_op jit(solution)/shard_map/all_gather | solution.py:32
  9.4 104.1 %all-reduce.7.cloned.1.call-start = ((), (), s32[]{:S(2)}) async-start(), calls=%async_computation.1 | async-start | bytes 2097152 | tf_op jit(solution)/shard_map/psum | solution.py:48
  53.5 3.2 copy-start
  60.2 120.9 %all-reduce.9.cloned.1.call-start = ((), (), s32[]{:S(2)}) async-start(), calls=%async_computation.2 | async-start | bytes 2097152 | tf_op jit(solution)/shard_map/psum | solution.py:61
  122.4 127.6 %all-reduce.11.cloned.1.call-start = ((), (), s32[]{:S(2)}) async-start(), calls=%async_computation.3 | async-start | bytes 2097152 | tf_op jit(solution)/shard_map/psum | solution.py:48
  200.0 118.3 %all-reduce.13.cloned.1.call-start = ((), (), s32[]{:S(2)}) async-start(), calls=%async_computation.4 | async-start | bytes 2097152 | tf_op jit(solution)/shard_map/psum | solution.py:61
Sparse Core Ops, SparseCore 0:
  9.6 36.0 all-gather.2
  60.3 52.8 all-reduce.6
  122.5 58.5 all-reduce.8
  200.2 49.8 all-reduce.10
  259.0 59.2 all-reduce.12
where the time goes:
time: 338 us
  waiting for transfers between devices  169 us (50%)
  blocking collectives  102 us (30%)
  matrix products  36.3 us (11%)
  between operations  13.9 us (4%)
  other arithmetic  12.6 us (4%)
    psum x2, waiting for transfers between devices, local(): image = lax.psum(partial_rows, 'lm')  118 us
    psum x2, waiting for transfers between devices, local(): lax.psum(jnp.einsum('rl,rv->lv', build_tile, group_weighted, preferred_el...  50 us
    psum x1, blocking collectives, local(): totals = lax.psum(jnp.sum(weighted_full, axis=0), ('grp', 'lm'))  40.3 us
    psum x2, blocking collectives, local(): lax.psum((jnp.sum(image * image, axis=0), jnp.sum(weights[:, None] * imag...  19.7 us
    all_gather x1, blocking collectives, local(): lax.all_gather(weighted_full.astype(jnp.bfloat16), 'lm', axis=0, tiled=True)  17.3 us
    dot_general x2, matrix products, local(): jnp.dot(build_tile, side_b, preferred_element_type=jnp.float32)  14.1 us
    all_gather x1, blocking collectives, local(): lax.all_gather(row_weight.astype(jnp.bfloat16), 'lm', axis=0, tiled=True)  13.5 us
    psum x1, blocking collectives, local(): mean_sum, weight_sum = lax.psum((sums, jnp.sum(weights)), 'grp')  11.7 us
  transfers between devices with their start and end apart: 5, of which 4 were waited for; matrix products, arithmetic and copies ran while one was open for 1% of the time, Pallas kernels for 0%

commit v1 on v0

--- a/solution.py
+++ b/solution.py
@@ -41,7 +41,7 @@
     means = mean_sum / weight_sum
     vectors = start_vectors
     weighted_full = row_weight[:, None] * vectors
-    totals = lax.psum(jnp.sum(weighted_full, axis=0), ("grp", "lm"))
+    totals = jnp.sum(lax.all_gather(jnp.sum(weighted_full, axis=0), ("grp", "lm")), axis=0)
     group_weighted = lax.all_gather(weighted_full.astype(jnp.bfloat16), "lm", axis=0, tiled=True)
     for step in range(ITERS):
         side = (

time: 338 us -> 338 us (level)
    psum x1 -> x0, blocking collectives: 40.3 us -> none  [local(): totals = lax.psum(jnp.sum(weighted_full, axis=0), ('grp', 'lm'))]
    all_gather x0 -> x1, blocking collectives: none -> 40 us  [local(): lax.all_gather(jnp.sum(weighted_full, axis=0), ('grp', 'lm'))]
  transfers between devices with their start and end apart: 5 -> 5, of which waited for: 4 -> 5; matrix products, arithmetic and copies ran while one was open for 1% -> 2% of each run, Pallas kernels for 0% -> 0%
where the time goes in v1:
time: 338 us; the launch traced here: 337 us
  waiting for transfers between devices  172 us (51%)
  blocking collectives  99.1 us (29%)
  matrix products  36.2 us (11%)
  between operations  13.9 us (4%)
  other arithmetic  12.7 us (4%)
    psum x2, waiting for transfers between devices, local(): image = lax.psum(partial_rows, 'lm')  118 us
    psum x2, waiting for transfers between devices, local(): lax.psum(jnp.einsum('rl,rv->lv', build_tile, group_weighted, preferred_el...  52.3 us
    all_gather x1, blocking collectives, local(): lax.all_gather(jnp.sum(weighted_full, axis=0), ('grp', 'lm'))  40 us
    psum x2, blocking collectives, local(): lax.psum((jnp.sum(image * image, axis=0), jnp.sum(weights[:, None] * imag...  19.7 us
    all_gather x1, blocking collectives, local(): lax.all_gather(weighted_full.astype(jnp.bfloat16), 'lm', axis=0, tiled=True)  17.3 us
    dot_general x2, matrix products, local(): jnp.dot(build_tile, side_b, preferred_element_type=jnp.float32)  14.1 us
    all_gather x1, blocking collectives, local(): lax.all_gather(row_weight.astype(jnp.bfloat16), 'lm', axis=0, tiled=True)  13.5 us
    dot_general x2, matrix products, local(): jnp.einsum('rl,rv->lv', build_tile, group_weighted, preferred_element_typ...  10.7 us
  transfers between devices with their start and end apart: 5, of which 5 were waited for; matrix products, arithmetic and copies ran while one was open for 2% of the time, Pallas kernels for 0%

profile of v1, /device:TPU:0, one launch (start us, length us, event | category | flops | bytes accessed | tf_op | source)
XLA Modules:
  0.0 337.1 jit_solution(10633857802084797743)
XLA Ops:
  6.5 0.0 all-gather.5.cloned.1.call-start
  6.5 1.1 fusion.8
  7.6 1.8 fusion.9
  9.4 0.0 all-gather.5.cloned.1.call-update
  9.4 0.0 all-reduce.7.cloned.1.call-start
  9.5 0.7 convert_element_type.35
  10.2 13.5 %all-gather.1 = bf16[8,1,256]{2,1,0:T(2,128)(2,1)S(1)} all-gather(bf16[1,1,256]{2,1,0:T(2,128)(2,1)S(1)} %reshape.22), channel_id=1, replica_groups=mesh['grp'=4,'lm'=8] {'lm'}, dimensions={0}, use_global_device_ids=true | all-gather | bytes 4608 | tf_op jit(solution)/shard_map/all_gather | solution.py:33
  24.3 2.1 fusion.1
  26.4 1.0 multiply_reduce_fusion.4
  27.4 17.3 %all_gather.17 = bf16[2048,128]{1,0:T(8,128)(2,1)S(1)} all-gather(bf16[256,128]{1,0:T(8,128)(2,1)S(1)} %get-tuple-element.14), channel_id=1, replica_groups=mesh['grp'=4,'lm'=8] {'lm'}, dimensions={0}, use_global_device_ids=true | all-gather | bytes 589824 | tf_op jit(solution)/shard_map/all_gather | solution.py:45
  44.7 1.0 all-gather.5.cloned.1.call-done
  45.7 7.8 %multiply_reduce_fusion = (f32[2048]{0:T(1024)S(1)}, bf16[2048,2048]{1,0:T(8,128)(2,1)S(1)}) fusion(f32[2048]{0:T(1024)S(1)} %bitcast.20, f32[]{:T(128)} %bitcast.17, bf16[2048,512]{1,0:T(8,128)(2,1)} %all-gather.5.cloned.1.call-done, bf16[2048,512]{1,0:T(8,128)(2,1)} %param.6, f32[2048]{0:T(1024)S(1)} %add_rsqrt_fusion), kind=kOutput, calls=%fused_computation | convolution fusion | flops 4314888192 | bytes 12607492 | tf_op jit(solution)/shard_map/rd,ld->rl/dot_general | solution.py:16
  53.5 0.0 copy-start
  53.5 3.2 copy-done
  56.7 3.4 %fusion.14 = f32[2048,128]{1,0:T(8,128)} fusion(bf16[2048,2048]{1,0:T(8,128)(2,1)S(1)} %get-tuple-element.12, bf16[2048,128]{1,0:T(8,128)(2,1)S(1)} %all_gather.17), kind=kOutput, calls=%fused_computation.38 | convolution fusion | flops 1073741824 | bytes 9961472 | tf_op jit(solution)/shard_map/rl,rv->lv/dot_general | solution.py:49
  60.1 0.0 all-reduce.7.cloned.1.call-update
  60.1 0.0 all-reduce.9.cloned.1.call-start
  60.2 40.0 %all-gather.2 = f32[32,1,128]{2,1,0:T(1,128)S(1)} all-gather(f32[1,1,128]{2,1,0:T(1,128)S(1)} %bitcast.25), channel_id=2, replica_groups=mesh['grp'=4,'lm'=8] {'grp','lm'}, dimensions={0}, use_global_device_ids=true | all-gather | bytes 16896 | tf_op jit(solution)/shard_map/all_gather | solution.py:44
  100.2 0.1 reduce_sum.86
  100.2 0.6 convert_reduce_fusion
  100.8 8.6 %all-reduce.1 = (f32[2048]{0:T(1024)S(1)}, f32[]{:T(128)}) all-reduce(f32[2048]{0:T(1024)S(1)} %get-tuple-element.11, f32[]{:T(128)} %convert_reduce_fusion), channel_id=1, replica_groups=mesh['grp'=4,'lm'=8] {'grp'}, use_global_device_ids=true, to_apply=%region_4.0 | all-reduce | flops 2049 | bytes 16392 | tf_op jit(solution)/shard_map/psum | solution.py:40
  109.5 0.6 broadcast_divide_fusion
  110.1 2.4 all-reduce.7.cloned.1.call-done
  112.5 1.8 convolution_bitcast_fusion.1
  114.3 7.1 %fusion.4 = f32[2048,128]{1,0:T(8,128)} fusion(bf16[2048,2048]{1,0:T(8,128)(2,1)} %copy-done, f32[128]{0:T(128)S(1)} %convolution_bitcast_fusion.1, f32[2048]{0:T(1024)S(1)} %bitcast.21, f32[2048,128]{1,0:T(8,128)} %all-reduce.7.cloned.1.call-done, f32[128]{0:T(128)S(1)} %reduce_sum.86, f32[2048]{0:T(1024)S(1)} %broadcast_divide_fusion), kind=kOutput, calls=%fused_computation.10 | convolution fusion | flops 1075052544 | bytes 10503168 | tf_op jit(solution)/shard_map/dot_general | solution.py:59
  121.4 0.0 all-reduce.9.cloned.1.call-update
  121.4 0.0 all-reduce.11.cloned.1.call-start
  121.5 59.0 %all-reduce.9.cloned.1.call-done = f32[2048,128]{1,0:T(8,128)} async-done(((f32[2048,128]{1,0:T(8,128)}), f32[2048,128]{1,0:T(8,128)}) %all-reduce.9.cloned.1.call-update) | async-done | bytes 1048592 | tf_op jit(solution)/shard_map/psum | solution.py:61
  180.4 1.6 multiply_reduce_fusion.2
  182.0 10.0 %all-reduce = (f32[128]{0:T(128)S(1)}, f32[128]{0:T(128)S(1)}) all-reduce(f32[128]{0:T(128)S(1)} %get-tuple-element.6, f32[128]{0:T(128)S(1)} %get-tuple-element.5), channel_id=1, replica_groups=mesh['grp'=4,'lm'=8] {'grp'}, use_global_device_ids=true, to_apply=%region_11.0 | all-reduce | flops 256 | bytes 2048 | tf_op jit(solution)/shard_map/psum | solution.py:62
  192.0 7.3 %fusion.10 = f32[2048,128]{1,0:T(8,128)} fusion(bf16[2048,2048]{1,0:T(8,128)(2,1)} %copy-done, f32[2048,128]{1,0:T(8,128)} %all-reduce.9.cloned.1.call-done, f32[128]{0:T(128)S(1)} %get-tuple-element.16, f32[2048]{0:T(1024)S(1)} %bitcast.23), kind=kOutput, calls=%fused_computation.25 | convolution fusion | flops 1074528256 | bytes 10494464 | tf_op jit(solution)/shard_map/rl,rv->lv/dot_general | solution.py:49
  199.3 0.0 all-reduce.11.cloned.1.call-update
  199.4 0.0 all-reduce.13.cloned.1.call-start
  199.4 49.9 %all-reduce.11.cloned.1.call-done = f32[2048,128]{1,0:T(8,128)} async-done(((f32[2048,128]{1,0:T(8,128)}), f32[2048,128]{1,0:T(8,128)}) %all-reduce.11.cloned.1.call-update) | async-done | bytes 1048592 | tf_op jit(solution)/shard_map/psum | solution.py:48
  249.3 1.8 convolution_bitcast_fusion
  251.1 7.1 %fusion.3 = f32[2048,128]{1,0:T(8,128)} fusion(bf16[2048,2048]{1,0:T(8,128)(2,1)} %copy-done, f32[128]{0:T(128)S(1)} %convolution_bitcast_fusion, f32[2048]{0:T(1024)S(1)} %bitcast.24, f32[2048,128]{1,0:T(8,128)} %all-reduce.11.cloned.1.call-done, f32[128]{0:T(128)S(1)} %get-tuple-element.15, f32[2048]{0:T(1024)S(1)} %broadcast_divide_fusion), kind=kOutput, calls=%fused_computation.8 | convolution fusion | flops 1075052544 | bytes 10503168 | tf_op jit(solution)/shard_map/dot_general | solution.py:59
  258.2 0.0 all-reduce.13.cloned.1.call-update
  258.2 59.5 %all-reduce.13.cloned.1.call-done = f32[2048,128]{1,0:T(8,128)} async-done(((f32[2048,128]{1,0:T(8,128)}), f32[2048,128]{1,0:T(8,128)}) %all-reduce.13.cloned.1.call-update) | async-done | bytes 1048592 | tf_op jit(solution)/shard_map/psum | solution.py:61
  317.7 1.5 multiply_reduce_fusion.1
  319.2 9.8 %psum.71 = f32[128]{0:T(128)S(1)} all-reduce(f32[128]{0:T(128)S(1)} %multiply_reduce_fusion.1), channel_id=1, replica_groups=mesh['grp'=4,'lm'=8] {'grp'}, use_global_device_ids=true, to_apply=%region_17.0 | all-reduce | flops 128 | bytes 1024 | tf_op jit(solution)/shard_map/psum | solution.py:62
  329.0 1.6 dynamic-slice_divide_fusion
  (6 shorter events, 0.1 us)
Async XLA Ops:
  6.5 39.1 %all-gather.5.cloned.1.call-start = ((), (), s32[]{:S(2)}) async-start(), calls=%async_computation | async-start | bytes 2359296 | tf_op jit(solution)/shard_map/all_gather | solution.py:32
  9.4 103.1 %all-reduce.7.cloned.1.call-start = ((), (), s32[]{:S(2)}) async-start(), calls=%async_computation.1 | async-start | bytes 2097152 | tf_op jit(solution)/shard_map/psum | solution.py:48
  53.5 3.2 copy-start
  60.1 120.3 %all-reduce.9.cloned.1.call-start = ((), (), s32[]{:S(2)}) async-start(), calls=%async_computation.2 | async-start | bytes 2097152 | tf_op jit(solution)/shard_map/psum | solution.py:61
  121.4 127.9 %all-reduce.11.cloned.1.call-start = ((), (), s32[]{:S(2)}) async-start(), calls=%async_computation.3 | async-start | bytes 2097152 | tf_op jit(solution)/shard_map/psum | solution.py:48
  199.4 118.3 %all-reduce.13.cloned.1.call-start = ((), (), s32[]{:S(2)}) async-start(), calls=%async_computation.4 | async-start | bytes 2097152 | tf_op jit(solution)/shard_map/psum | solution.py:61
Sparse Core Ops, SparseCore 0:
  9.6 36.0 all-gather.4
  60.2 52.2 all-reduce.6
  121.6 58.8 all-reduce.8
  199.5 49.7 all-reduce.10
  258.3 59.2 all-reduce.12
